TPU v7x, 512 devices: a whole 4x8x8 slice. The times are simulated.
512 devices in a mesh: lon: 64 (over z_lo, x, y), lat: 8 (over z_hi, core).
Axes of the slice: x: 4, y: 8, z: 8 (z_hi: 4, z_lo: 2; z = z_hi * 2 + z_lo), core: 2. Of those that a mesh axis runs over, the one named last changes fastest.
Arguments:
- thermal_anomaly: float32 [16, 512, 1024], P(None, 'lon', 'lat'), may hold values from -6 to 6
- saltiness_anomaly: float32 [16, 512, 1024], P(None, 'lon', 'lat'), may hold values from -6 to 6
- zonal_current: float32 [16, 512, 1024], P(None, 'lon', 'lat'), may hold values from -3 to 3
- meridional_current: float32 [16, 512, 1024], P(None, 'lon', 'lat'), may hold values from -3 to 3
- bottom_ocean_layer: int32 [512, 1024], P('lon', 'lat'), may hold values from 0 to 16
- seam_axis_meridian: int32 [1], replicated, may hold values from 0 to 1023
- interface_diffusivity: float32 [15, 512, 1024], P(None, 'lon', 'lat'), may hold values from 0.1 to 10
- atmospheric_forcing: float32 [2, 512, 1024], P(None, 'lon', 'lat'), may hold values from -6 to 6
Outputs:
- temperature_next: float32 [16, 512, 1024], P(None, 'lon', 'lat')
- salinity_next: float32 [16, 512, 1024], P(None, 'lon', 'lat')
- zonal_next: float32 [16, 512, 1024], P(None, 'lon', 'lat')
- meridional_next: float32 [16, 512, 1024], P(None, 'lon', 'lat')
Inputs may be any that keep to these rules, and one draw needn't show every extreme that they name: `seam_axis_meridian`: an even code folds about a cell centre, an odd one about a cell corner.
All inputs are finite; a program needn't handle non-finite values.
Results may differ from a plain program's by a relative error of at most 0.0003.
Values sent between devices are 32-bit elements; how exact they have to be, the bound alone decides.
A program may use at most 64 MiB of HBM per device.

v0:
```python
import jax
import jax.numpy as jnp
from jax import lax
from jax.sharding import PartitionSpec as P

TIME_STEP = 0.2
TRACER_DIFF = 0.2
MOMENTUM_VISC = 0.2
THERMAL_EXPANSION = 0.5
HALINE_CONTRACTION = 0.4
WIND_GAIN = 2.0
VERTICAL_VISC = 1.0
NEIGHBOURS = ((1, 0), (-1, 0), (0, 1), (0, -1))


def padded(block, sides, width):
    for axis, dim in sides:
        count = lax.axis_size(axis)
        forward = [(i, i + 1) for i in range(count - 1)]
        forward.append((count - 1, 0))
        backward = [(target, source) for source, target in forward]
        low = lax.ppermute(
            lax.slice_in_dim(block, block.shape[dim] - width, None, axis=dim), axis, forward
        )
        high = lax.ppermute(lax.slice_in_dim(block, 0, width, axis=dim), axis, backward)
        block = jnp.concatenate([low, block, high], axis=dim)
    return block


def implicit(right_side, coupling):
    count = right_side.shape[-3]
    ratios = []
    values = []
    for level_k in range(count):
        below = coupling[level_k] if level_k < count - 1 else 0.0
        above = coupling[level_k - 1] if level_k > 0 else 0.0
        if level_k == 0:
            denom = 1.0 + below
            values.append(right_side[..., 0, :, :] / denom)
        else:
            denom = 1.0 + above + below + above * ratios[level_k - 1]
            values.append((right_side[..., level_k, :, :] + above * values[level_k - 1]) / denom)
        ratios.append(-below / denom)
    result = [values[count - 1]]
    for level_k in range(count - 2, -1, -1):
        result.insert(0, values[level_k] - ratios[level_k] * result[0])
    return jnp.stack(result, axis=-3)


def choose_rows(source, fold_type, sign_column):
    upper = jnp.where(fold_type == 1, source[..., 2], source[..., 1])
    outer = jnp.where(fold_type == 1, source[..., 1], source[..., 0])
    return jnp.stack([upper, outer], axis=-1) * sign_column


def advance(grid_ext, interface_diffusivity, atmospheric_forcing, row_start, rows_total):
    layer_number = (grid_ext.shape[0] - 1) // 4
    cols_n = grid_ext.shape[1] - 4
    rows_n = grid_ext.shape[2] - 4

    def view(source_array, shift_x, shift_y):
        return source_array[
            ..., 2 + shift_x : 2 + shift_x + cols_n, 2 + shift_y : 2 + shift_y + rows_n
        ]

    tracers = grid_ext[: 2 * layer_number].reshape(2, layer_number, cols_n + 4, rows_n + 4)
    zonal = grid_ext[2 * layer_number : 3 * layer_number]
    merid = grid_ext[3 * layer_number : 4 * layer_number]
    depth_count = grid_ext[4 * layer_number]
    level_ids = jnp.arange(layer_number).astype(jnp.float32)[:, None, None]
    wet_mask = jnp.where(level_ids < depth_count[None], 1.0, 0.0).astype(jnp.float32)

    def face_x(shift_x):
        interp = (
            7.0 * (view(tracers, shift_x, 0) + view(tracers, shift_x + 1, 0))
            - (view(tracers, shift_x - 1, 0) + view(tracers, shift_x + 2, 0))
        ) / 12.0
        return (
            view(zonal, shift_x, 0)
            * view(wet_mask, shift_x, 0)
            * view(wet_mask, shift_x + 1, 0)
            * interp
        )

    def face_y(shift_y):
        interp = (
            7.0 * (view(tracers, 0, shift_y) + view(tracers, 0, shift_y + 1))
            - (view(tracers, 0, shift_y - 1) + view(tracers, 0, shift_y + 2))
        ) / 12.0
        return (
            view(merid, 0, shift_y)
            * view(wet_mask, 0, shift_y)
            * view(wet_mask, 0, shift_y + 1)
            * interp
        )

    advect = -(face_x(0) - face_x(-1)) - (face_y(0) - face_y(-1))
    centre = view(tracers, 0, 0)
    wet_centre = view(wet_mask, 0, 0)
    spread = jnp.zeros_like(centre)
    for shift_x, shift_y in NEIGHBOURS:
        spread = spread + view(wet_mask, shift_x, shift_y) * wet_centre * (
            view(tracers, shift_x, shift_y) - centre
        )
    tracer_star = centre + TIME_STEP * (advect + TRACER_DIFF * spread) * wet_centre
    buoyancy = (
        THERMAL_EXPANSION * grid_ext[:layer_number]
        - HALINE_CONTRACTION * grid_ext[layer_number : 2 * layer_number]
    ) * wet_mask
    pressure = jnp.cumsum(buoyancy, axis=0) - 0.5 * buoyancy
    u_mask = wet_centre * view(wet_mask, 1, 0)
    v_mask = wet_centre * view(wet_mask, 0, 1)
    row_ids = (row_start + jnp.arange(rows_n)).astype(jnp.float32)
    cor_u = 2.0 * (row_ids + 0.5) / rows_total - 1.0
    cor_v = 2.0 * (row_ids + 1.0) / rows_total - 1.0
    v_at_u = 0.25 * (
        view(merid, 0, 0) + view(merid, 0, -1) + view(merid, 1, 0) + view(merid, 1, -1)
    )
    u_at_v = 0.25 * (
        view(zonal, 0, 0) + view(zonal, -1, 0) + view(zonal, 0, 1) + view(zonal, -1, 1)
    )
    u_centre = view(zonal, 0, 0)
    v_centre = view(merid, 0, 0)
    u_visc = jnp.zeros_like(u_centre)
    v_visc = jnp.zeros_like(v_centre)
    for shift_x, shift_y in NEIGHBOURS:
        u_visc = u_visc + view(wet_mask, shift_x, shift_y) * view(
            wet_mask, shift_x + 1, shift_y
        ) * u_mask * (view(zonal, shift_x, shift_y) - u_centre)
        v_visc = v_visc + view(wet_mask, shift_x, shift_y) * view(
            wet_mask, shift_x, shift_y + 1
        ) * v_mask * (view(merid, shift_x, shift_y) - v_centre)
    u_star = (
        u_centre
        + TIME_STEP
        * (cor_u * v_at_u - (view(pressure, 1, 0) - view(pressure, 0, 0)) + MOMENTUM_VISC * u_visc)
    ) * u_mask
    v_star = (
        v_centre
        + TIME_STEP
        * (-cor_v * u_at_v - (view(pressure, 0, 1) - view(pressure, 0, 0)) + MOMENTUM_VISC * v_visc)
    ) * v_mask
    u_star = u_star.at[0].add(TIME_STEP * WIND_GAIN * atmospheric_forcing[0] * u_mask[0])
    v_star = v_star.at[0].add(TIME_STEP * WIND_GAIN * atmospheric_forcing[1] * v_mask[0])
    tracer_next = implicit(
        tracer_star, TIME_STEP * interface_diffusivity * wet_centre[:-1] * wet_centre[1:]
    )
    u_next = implicit(u_star, TIME_STEP * VERTICAL_VISC * u_mask[:-1] * u_mask[1:])
    v_next = implicit(v_star, TIME_STEP * VERTICAL_VISC * v_mask[:-1] * v_mask[1:])
    return (tracer_next[0], tracer_next[1], u_next, v_next)


def shards(
    thermal_anomaly,
    saltiness_anomaly,
    zonal_current,
    meridional_current,
    bottom_ocean_layer,
    seam_axis_meridian,
    interface_diffusivity,
    atmospheric_forcing,
):
    layer_number = thermal_anomaly.shape[0]
    block_meridian_number = thermal_anomaly.shape[1]
    block_parallel_number = thermal_anomaly.shape[2]
    combined_arrays = jnp.concatenate(
        [
            thermal_anomaly,
            saltiness_anomaly,
            zonal_current,
            meridional_current,
            bottom_ocean_layer.astype(jnp.float32)[None],
        ],
        axis=0,
    )
    lon_count = lax.axis_size("lon")
    lat_count = lax.axis_size("lat")
    lon_index = lax.axis_index("lon")
    lat_index = lax.axis_index("lat")
    total_lon = block_meridian_number * lon_count
    fold_code = seam_axis_meridian[0]
    fold_type = jnp.mod(fold_code, 2)
    sign_column = jnp.concatenate(
        [
            jnp.ones((2 * layer_number,), jnp.float32),
            -jnp.ones((2 * layer_number,), jnp.float32),
            jnp.ones((1,), jnp.float32),
        ]
    )[:, None, None]
    top_rows = combined_arrays[:, :, block_parallel_number - 3 :]
    margin = 2
    first_col = lon_index * block_meridian_number - margin
    col_count = block_meridian_number + 2 * margin
    targets = jnp.mod(fold_code - (first_col + jnp.arange(col_count)), total_lon)
    piece = lax.all_gather(top_rows, "lon", axis=1, tiled=True)
    column_ids = jnp.arange(piece.shape[1])
    selector = jnp.where(column_ids[:, None] == targets[None, :], 1.0, 0.0).astype(jnp.float32)
    source = jnp.einsum("anr,nc->acr", piece, selector, precision=lax.Precision.HIGHEST)
    ghost = choose_rows(source, fold_type, sign_column)
    is_top = lat_index == lat_count - 1
    grid_ext = padded(combined_arrays, (("lon", 1), ("lat", 2)), 2)
    south_keep = jnp.where(
        jnp.logical_and(lat_index == 0, jnp.arange(block_parallel_number + 4) < 2), 0.0, 1.0
    ).astype(jnp.float32)
    grid_ext = grid_ext * south_keep
    grid_ext = jnp.where(
        is_top,
        jnp.concatenate([grid_ext[..., : block_parallel_number + 2], ghost], axis=2),
        grid_ext,
    )
    return advance(
        grid_ext,
        interface_diffusivity,
        atmospheric_forcing,
        lat_index * block_parallel_number,
        block_parallel_number * lat_count,
    )


def solution(mesh):
    placed = (
        P(None, "lon", "lat"),
        P(None, "lon", "lat"),
        P(None, "lon", "lat"),
        P(None, "lon", "lat"),
        P("lon", "lat"),
        P(),
        P(None, "lon", "lat"),
        P(None, "lon", "lat"),
    )
    return jax.shard_map(
        shards,
        mesh=mesh,
        in_specs=placed,
        out_specs=(
            P(None, "lon", "lat"),
            P(None, "lon", "lat"),
            P(None, "lon", "lat"),
            P(None, "lon", "lat"),
        ),
        check_vma=False,
    )
```

profile of v0, /device:TPU:201, one launch (start us, length us, event | category | flops | bytes accessed | tf_op | source)
XLA Modules:
  0.0 341.6 jit_solution(17473160580814597958)
XLA Ops:
  0.6 0.8 constant_dynamic-update-slice_fusion.4
  1.5 0.8 constant_dynamic-update-slice_fusion.3
  2.3 0.8 constant_dynamic-update-slice_fusion.2
  3.2 0.8 constant_dynamic-update-slice_fusion.1
  4.0 0.7 constant_dynamic-update-slice_fusion
  4.7 3.2 collective-permute-start
  8.0 2.1 collective-permute-start.1
  10.9 266.5 %all_gather.3 = f32[65,512,3]{2,1,0:T(8,128)} all-gather(f32[65,8,3]{2,1,0:T(8,128)S(1)} %slice.759), channel_id=1, replica_groups=mesh['lon'=64,'lat'=8] {'lon'}, dimensions={1}, use_global_device_ids=true | all-gather | bytes 405600 | tf_op jit(solution)/shard_map/all_gather | solution.py:195
  277.4 10.2 %copy.565 = f32[65,512,3]{0,1,2:T(8,128)S(1)} copy(f32[65,512,3]{2,1,0:T(8,128)} %all_gather.3) | data formatting | bytes 798720 | tf_op jit(solution)/shard_map/all_gather | solution.py:195
  287.6 0.5 convolution_bitcast_fusion
  288.8 38.1 %collective-permute-start.2 = (f32[65,12,2]{0,2,1:T(2,128)S(1)}, f32[65,12,2]{0,2,1:T(2,128)S(1)}, u32[]{:S(2)}, u32[]{:S(2)}) collective-permute-start(f32[65,12,2]{0,2,1:T(2,128)S(1)} %copy.561), channel_id=1, source_target_pairs={{0,1},{1,2},{2,3},{3,4},{4,5},{5,6},{6,7},{7,0},{8,9},{9,10},{10,1... | collective-permute-start | bytes 18728 | tf_op jit(solution)/shard_map/ppermute | solution.py:22
  327.1 1.9 collective-permute-start.3
  329.0 0.3 copy.569
  329.4 0.3 copy.563
  329.7 4.5 %collective-permute-done.3 = f32[65,12,2]{0,2,1:T(2,128)S(1)} collective-permute-done((f32[65,12,2]{0,2,1:T(2,128)S(1)}, f32[65,12,2]{0,2,1:T(2,128)S(1)}, u32[]{:S(2)}, u32[]{:S(2)}) %collective-permute-start.3) | collective-permute-done | bytes 6272 | tf_op jit(solution)/shard_map/ppermute | solution.py:25
  334.2 0.3 copy.564
  334.6 0.8 maximum_multiply_fusion
  335.3 0.3 maximum_select_fusion
  335.9 0.4 fusion.40
  336.4 0.4 fusion.27
  337.1 0.4 copy-done.2
  339.3 0.4 fusion.9
  340.3 0.7 copy.582
  341.0 0.7 copy.583
  (100 shorter events, 3.6 us)
Async XLA Ops:
  4.7 283.5 %collective-permute-start = (f32[65,2,128]{2,1,0:T(2,128)S(1)}, f32[65,2,128]{2,1,0:T(2,128)S(1)}, u32[]{:S(2)}, u32[]{:S(2)}) collective-permute-start(f32[65,2,128]{2,1,0:T(2,128)S(1)} %get-tuple-element.201), channel_id=1, source_target_pairs={{0,8},{8,16},{16,24},{24,32},{32,40},{40,48},{48,56},{56,64},{64,7... | collective-permute-start | bytes 199688 | tf_op jit(solution)/shard_map/ppermute | solution.py:22
  8.0 280.2 %collective-permute-start.1 = (f32[65,2,128]{2,1,0:T(2,128)S(1)}, f32[65,2,128]{2,1,0:T(2,128)S(1)}, u32[]{:S(2)}, u32[]{:S(2)}) collective-permute-start(f32[65,2,128]{2,1,0:T(2,128)S(1)} %get-tuple-element.202), channel_id=1, source_target_pairs={{8,0},{16,8},{24,16},{32,24},{40,32},{48,40},{56,48},{64,56},{72,6... | collective-permute-start | bytes 199688 | tf_op jit(solution)/shard_map/ppermute | solution.py:25
  277.4 10.8 %copy-start.3 = (f32[65]{0:T(128)S(1)}, f32[65]{0:T(128)}, u32[]{:S(2)}) copy-start(f32[65]{0:T(128)} %constant.125.clone.1) | copy-start | bytes 784
  288.8 40.6 %collective-permute-start.2 = (f32[65,12,2]{0,2,1:T(2,128)S(1)}, f32[65,12,2]{0,2,1:T(2,128)S(1)}, u32[]{:S(2)}, u32[]{:S(2)}) collective-permute-start(f32[65,12,2]{0,2,1:T(2,128)S(1)} %copy.561), channel_id=1, source_target_pairs={{0,1},{1,2},{2,3},{3,4},{4,5},{5,6},{6,7},{7,0},{8,9},{9,10},{10,1... | collective-permute-start | bytes 18728 | tf_op jit(solution)/shard_map/ppermute | solution.py:22
  327.1 7.1 %collective-permute-start.3 = (f32[65,12,2]{0,2,1:T(2,128)S(1)}, f32[65,12,2]{0,2,1:T(2,128)S(1)}, u32[]{:S(2)}, u32[]{:S(2)}) collective-permute-start(f32[65,12,2]{0,2,1:T(2,128)S(1)} %copy.562), channel_id=1, source_target_pairs={{1,0},{2,1},{3,2},{4,3},{5,4},{6,5},{7,6},{0,7},{9,8},{10,9},{11,1... | collective-permute-start | bytes 18728 | tf_op jit(solution)/shard_map/ppermute | solution.py:25
  335.6 1.4 copy-start
  336.8 0.7 copy-start.2
  337.0 1.2 copy-start.1
  337.8 1.0 copy-start.4
  338.0 1.1 slice-start
  338.3 1.0 copy-start.5
where the time goes:
time: 342 us
  blocking collectives  267 us (78%)
  starting transfers between devices  45.3 us (13%)
  local copies, waits for them, and re-layouts  18.1 us (5%)
  other arithmetic  4.76 us (1%)
  waiting for transfers between devices  4.49 us (1%)
    all_gather x1, blocking collectives, shards(): piece = lax.all_gather(top_rows, 'lon', axis=1, tiled=True)  267 us
    ppermute x2, starting transfers between devices, padded(): lax.ppermute(lax.slice_in_dim(block, block.shape[dim] - width, None, axis...  41.3 us
    all_gather x1, local copies, waits for them, and re-layouts, shards(): piece = lax.all_gather(top_rows, 'lon', axis=1, tiled=True)  10.2 us
  transfers between devices with their start and end apart: 4, of which 1 were waited for; matrix products, arithmetic and copies ran while one was open for 3% of the time, Pallas kernels for 0%

commit v1 on v0

--- a/solution.py
+++ b/solution.py
@@ -192,7 +192,8 @@
     first_col = lon_index * block_meridian_number - margin
     col_count = block_meridian_number + 2 * margin
     targets = jnp.mod(fold_code - (first_col + jnp.arange(col_count)), total_lon)
-    piece = lax.all_gather(top_rows, "lon", axis=1, tiled=True)
+    a_now = jnp.stack([top_rows] * lax.axis_size("lon"))
+    piece = jnp.concatenate(lax.all_to_all(a_now, "lon", 0, 0), axis=1)
     column_ids = jnp.arange(piece.shape[1])
     selector = jnp.where(column_ids[:, None] == targets[None, :], 1.0, 0.0).astype(jnp.float32)
     source = jnp.einsum("anr,nc->acr", piece, selector, precision=lax.Precision.HIGHEST)

time: 342 us -> 55.8 us (0.16)
  the two profiles are of different devices: /device:TPU:201 before, /device:TPU:128 now
where the time goes in v1:
time: 55.8 us; the launch traced here: 55.2 us
  starting transfers between devices  23.8 us (43%)
  waiting for transfers between devices  16.3 us (29%)
  local copies, waits for them, and re-layouts  8.22 us (15%)
  other arithmetic  4.43 us (8%)
  between operations  2.02 us (4%)
    all_to_all x1, waiting for transfers between devices, shards(): piece = jnp.concatenate(lax.all_to_all(a_now, 'lon', 0, 0), axis=1)  12.8 us
    ppermute x2, starting transfers between devices, padded(): lax.ppermute(lax.slice_in_dim(block, 0, width, axis=dim), axis, backward)  9.73 us
    all_to_all x1, starting transfers between devices, shards(): piece = jnp.concatenate(lax.all_to_all(a_now, 'lon', 0, 0), axis=1)  8.13 us
    ppermute x2, starting transfers between devices, padded(): lax.ppermute(lax.slice_in_dim(block, block.shape[dim] - width, None, axis...  5.89 us
    unnamed x37, local copies, waits for them, and re-layouts  4.57 us
    ppermute x2, waiting for transfers between devices, padded(): lax.ppermute(lax.slice_in_dim(block, block.shape[dim] - width, None, axis...  3.49 us
  transfers between devices with their start and end apart: 5, of which 2 were waited for; matrix products, arithmetic and copies ran while one was open for 6% of the time, Pallas kernels for 0%

profile of v1, /device:TPU:128, one launch (start us, length us, event | category | flops | bytes accessed | tf_op | source)
XLA Modules:
  0.0 55.2 jit_solution(7991426174527265181)
XLA Ops:
  0.6 0.8 %constant_dynamic-update-slice_fusion.4 = f32[65,8,128]{2,1,0:T(8,128)S(1)} fusion(f32[16,8,128]{2,1,0:T(8,128)} %param.12), kind=kLoop, calls=%fused_computation.37 | loop fusion | bytes 131072
  1.5 0.8 %constant_dynamic-update-slice_fusion.3 = f32[65,8,128]{2,1,0:T(8,128)S(1)} fusion(f32[65,8,128]{2,1,0:T(8,128)S(1)} %constant_dynamic-update-slice_fusion.4, f32[16,8,128]{2,1,0:T(8,128)} %param.13), kind=kLoop, calls=%fused_computation.36 | loop fusion | bytes 131072
  2.3 0.8 %constant_dynamic-update-slice_fusion.2 = f32[65,8,128]{2,1,0:T(8,128)S(1)} fusion(f32[65,8,128]{2,1,0:T(8,128)S(1)} %constant_dynamic-update-slice_fusion.3, f32[16,8,128]{2,1,0:T(8,128)} %param.14), kind=kLoop, calls=%fused_computation.35 | loop fusion | bytes 131072
  3.2 0.8 %constant_dynamic-update-slice_fusion.1 = f32[65,8,128]{2,1,0:T(8,128)S(1)} fusion(f32[65,8,128]{2,1,0:T(8,128)S(1)} %constant_dynamic-update-slice_fusion.2, f32[16,8,128]{2,1,0:T(8,128)} %param.15), kind=kLoop, calls=%fused_computation.34 | loop fusion | bytes 131072
  4.0 0.7 %constant_dynamic-update-slice_fusion = f32[65,8,128]{2,1,0:T(8,128)S(1)} fusion(f32[65,8,128]{2,1,0:T(8,128)S(1)} %constant_dynamic-update-slice_fusion.1, s32[8,128]{1,0:T(8,128)} %param.16), kind=kLoop, calls=%fused_computation.33 | loop fusion | flops 1024 | bytes 8192 | tf_op jit(solution)/shard_map/concatenate | solution.py:166
  4.7 3.5 %collective-permute-start = (f32[65,2,128]{2,1,0:T(2,128)S(1)}, f32[65,2,128]{2,1,0:T(2,128)S(1)}, u32[]{:S(2)}, u32[]{:S(2)}) collective-permute-start(f32[65,2,128]{2,1,0:T(2,128)S(1)} %get-tuple-element.150), channel_id=1, source_target_pairs={{0,8},{8,16},{16,24},{24,32},{32,40},{40,48},{48,56},{56,64},{64,7... | collective-permute-start | bytes 199688 | tf_op jit(solution)/shard_map/ppermute | solution.py:22
  8.2 7.8 %collective-permute-start.1 = (f32[65,2,128]{2,1,0:T(2,128)S(1)}, f32[65,2,128]{2,1,0:T(2,128)S(1)}, u32[]{:S(2)}, u32[]{:S(2)}) collective-permute-start(f32[65,2,128]{2,1,0:T(2,128)S(1)} %get-tuple-element.151), channel_id=1, source_target_pairs={{8,0},{16,8},{24,16},{32,24},{40,32},{48,40},{56,48},{64,56},{72,6... | collective-permute-start | bytes 199688 | tf_op jit(solution)/shard_map/ppermute | solution.py:25
  16.4 1.0 %stack.10 = f32[64,65,8,3]{1,2,3,0:T(8,128)} broadcast(f32[65,8,3]{0,1,2:T(8,128)S(1)} %copy.21), dimensions={1,2,3} | broadcast | bytes 405600 | tf_op jit(solution)/shard_map/stack | solution.py:195
  17.3 8.1 %all-to-all-start = ((f32[64,65,8,3]{1,2,3,0:T(8,128)}), f32[64,65,8,3]{1,2,3,0:T(8,128)S(1)}, u32[]{:S(2)}, u32[]{:S(2)}) async-start(f32[64,65,8,3]{1,2,3,0:T(8,128)} %stack.10), calls=%async_computation | async-start | bytes 1572864 | tf_op jit(solution)/shard_map/all_to_all | solution.py:196
  27.0 1.9 %collective-permute-start.3 = (f32[65,12,2]{0,2,1:T(2,128)S(1)}, f32[65,12,2]{0,2,1:T(2,128)S(1)}, u32[]{:S(2)}, u32[]{:S(2)}) collective-permute-start(f32[65,12,2]{0,2,1:T(2,128)S(1)} %copy.18), channel_id=1, source_target_pairs={{1,0},{2,1},{3,2},{4,3},{5,4},{6,5},{7,6},{0,7},{9,8},{10,9},{11,1... | collective-permute-start | bytes 18728 | tf_op jit(solution)/shard_map/ppermute | solution.py:25
  28.9 2.4 %collective-permute-start.2 = (f32[65,12,2]{0,2,1:T(2,128)S(1)}, f32[65,12,2]{0,2,1:T(2,128)S(1)}, u32[]{:S(2)}, u32[]{:S(2)}) collective-permute-start(f32[65,12,2]{0,2,1:T(2,128)S(1)} %copy.17), channel_id=1, source_target_pairs={{0,1},{1,2},{2,3},{3,4},{4,5},{5,6},{6,7},{7,0},{8,9},{9,10},{10,1... | collective-permute-start | bytes 18728 | tf_op jit(solution)/shard_map/ppermute | solution.py:22
  31.3 3.5 %collective-permute-done.2 = f32[65,12,2]{0,2,1:T(2,128)S(1)} collective-permute-done((f32[65,12,2]{0,2,1:T(2,128)S(1)}, f32[65,12,2]{0,2,1:T(2,128)S(1)}, u32[]{:S(2)}, u32[]{:S(2)}) %collective-permute-start.2) | collective-permute-done | bytes 6272 | tf_op jit(solution)/shard_map/ppermute | solution.py:22
  34.8 0.3 copy.19
  35.2 0.3 copy.20
  35.5 0.8 %maximum_multiply_fusion = f32[65,12,132]{2,1,0:T(8,128)S(1)} fusion(f32[65,12,2]{2,1,0:T(8,128)S(1)} %copy.20, f32[65,2,128]{2,1,0:T(2,128)S(1)} %collective-permute-done.1, f32[65,8,128]{2,1,0:T(8,128)S(1)} %constant_dynamic-update-slice_fusion, f32[65,2,128]{2,1,0:T(2,128)S(1)} %collective-permute-done, f32[65,12,2]{2,1,0:T(8,128)S(1)} %copy.19, ...), kind=kLoop, calls=%fused_computation.2 | loop fusion | flops 514800 | bytes 824208 | tf_op jit(solution)/shard_map/mul | solution.py:206
  36.3 12.8 %all-to-all-done = f32[64,65,8,3]{1,2,3,0:T(8,128)S(1)} async-done(((f32[64,65,8,3]{1,2,3,0:T(8,128)}), f32[64,65,8,3]{1,2,3,0:T(8,128)S(1)}, u32[]{:S(2)}, u32[]{:S(2)}) %all-to-all-start) | async-done | bytes 399392 | tf_op jit(solution)/shard_map/all_to_all | solution.py:196
  49.1 0.5 convolution_bitcast_fusion
  49.6 0.3 copy.24
  50.0 0.3 maximum_select_fusion
  50.8 0.7 %copy-done.1 = f32[15,8,128]{2,1,0:T(8,128)S(1)} copy-done((f32[15,8,128]{2,1,0:T(8,128)S(1)}, f32[15,8,128]{2,1,0:T(8,128)}, u32[]{:S(2)}) %copy-start.1) | copy-done | bytes 61464
  51.7 0.4 fusion.29
  52.1 0.4 fusion.42
  53.7 0.3 fusion.11
  54.5 0.7 %slice_bitcast_fusion = (f32[16,8,128]{2,1,0:T(8,128)}, f32[16,8,128]{2,1,0:T(8,128)}) fusion(f32[2,16,8,128]{3,2,1,0:T(8,128)S(1)} %constant_dynamic-update-slice_fusion.5), kind=kLoop, calls=%fused_computation.126 | loop fusion | bytes 262144 | tf_op jit(solution)/shard_map/squeeze | solution.py:150
  (94 shorter events, 3.1 us)
Async XLA Ops:
  4.7 21.4 %collective-permute-start = (f32[65,2,128]{2,1,0:T(2,128)S(1)}, f32[65,2,128]{2,1,0:T(2,128)S(1)}, u32[]{:S(2)}, u32[]{:S(2)}) collective-permute-start(f32[65,2,128]{2,1,0:T(2,128)S(1)} %get-tuple-element.150), channel_id=1, source_target_pairs={{0,8},{8,16},{16,24},{24,32},{32,40},{40,48},{48,56},{56,64},{64,7... | collective-permute-start | bytes 199688 | tf_op jit(solution)/shard_map/ppermute | solution.py:22
  8.2 17.9 %collective-permute-start.1 = (f32[65,2,128]{2,1,0:T(2,128)S(1)}, f32[65,2,128]{2,1,0:T(2,128)S(1)}, u32[]{:S(2)}, u32[]{:S(2)}) collective-permute-start(f32[65,2,128]{2,1,0:T(2,128)S(1)} %get-tuple-element.151), channel_id=1, source_target_pairs={{8,0},{16,8},{24,16},{32,24},{40,32},{48,40},{56,48},{64,56},{72,6... | collective-permute-start | bytes 199688 | tf_op jit(solution)/shard_map/ppermute | solution.py:25
  17.3 31.8 %all-to-all-start = ((f32[64,65,8,3]{1,2,3,0:T(8,128)}), f32[64,65,8,3]{1,2,3,0:T(8,128)S(1)}, u32[]{:S(2)}, u32[]{:S(2)}) async-start(f32[64,65,8,3]{1,2,3,0:T(8,128)} %stack.10), calls=%async_computation | async-start | bytes 1572864 | tf_op jit(solution)/shard_map/all_to_all | solution.py:196
  27.0 8.2 %collective-permute-start.3 = (f32[65,12,2]{0,2,1:T(2,128)S(1)}, f32[65,12,2]{0,2,1:T(2,128)S(1)}, u32[]{:S(2)}, u32[]{:S(2)}) collective-permute-start(f32[65,12,2]{0,2,1:T(2,128)S(1)} %copy.18), channel_id=1, source_target_pairs={{1,0},{2,1},{3,2},{4,3},{5,4},{6,5},{7,6},{0,7},{9,8},{10,9},{11,1... | collective-permute-start | bytes 18728 | tf_op jit(solution)/shard_map/ppermute | solution.py:25
  28.9 5.9 %collective-permute-start.2 = (f32[65,12,2]{0,2,1:T(2,128)S(1)}, f32[65,12,2]{0,2,1:T(2,128)S(1)}, u32[]{:S(2)}, u32[]{:S(2)}) collective-permute-start(f32[65,12,2]{0,2,1:T(2,128)S(1)} %copy.17), channel_id=1, source_target_pairs={{0,1},{1,2},{2,3},{3,4},{4,5},{5,6},{6,7},{7,0},{8,9},{9,10},{10,1... | collective-permute-start | bytes 18728 | tf_op jit(solution)/shard_map/ppermute | solution.py:22
  35.5 14.1 %copy-start.3 = (f32[65]{0:T(128)S(1)}, f32[65]{0:T(128)}, u32[]{:S(2)}) copy-start(f32[65]{0:T(128)} %constant.125.clone.1) | copy-start | bytes 784
  50.3 1.9 %copy-start = (f32[65,12,132]{2,1,0:T(8,128)}, f32[65,12,132]{2,1,0:T(8,128)S(1)}, u32[]{:S(2)}) copy-start(f32[65,12,132]{2,1,0:T(8,128)S(1)} %maximum_select_fusion) | copy-start | bytes 1235524
  50.5 0.9 %copy-start.1 = (f32[15,8,128]{2,1,0:T(8,128)S(1)}, f32[15,8,128]{2,1,0:T(8,128)}, u32[]{:S(2)}) copy-start(f32[15,8,128]{2,1,0:T(8,128)} %param.18) | copy-start | bytes 184324
  52.1 0.7 %copy-start.2 = (f32[2,8,128]{2,1,0:T(8,128)S(1)}, f32[2,8,128]{2,1,0:T(8,128)}, u32[]{:S(2)}) copy-start(f32[2,8,128]{2,1,0:T(8,128)} %param.19) | copy-start | bytes 24580
  52.5 1.1 %slice-start = ((f32[65,12,132]{2,1,0:T(8,128)}), f32[32,12,132]{2,1,0:T(8,128)S(1)}, s32[]{:S(2)}) async-start(f32[65,12,132]{2,1,0:T(8,128)} %copy-done), calls=%async_computation.1 | async-start | bytes 1048576 | tf_op jit(solution)/shard_map/slice | solution.py:66
  53.2 0.8 %copy-start.4 = (f32[16,8,128]{2,1,0:T(8,128)}, f32[16,8,128]{2,1,0:T(8,128)S(1)}, u32[]{:S(2)}) copy-start(f32[16,8,128]{2,1,0:T(8,128)S(1)} %constant_dynamic-update-slice_fusion.21) | copy-start | bytes 196612
  53.6 0.6 %copy-start.5 = (f32[16,8,128]{2,1,0:T(8,128)}, f32[16,8,128]{2,1,0:T(8,128)S(1)}, u32[]{:S(2)}) copy-start(f32[16,8,128]{2,1,0:T(8,128)S(1)} %constant_dynamic-update-slice_fusion.37) | copy-start | bytes 196612
